TPU v7x, 32 devices: a whole 2x2x4 slice. The times are simulated.
32 devices in a mesh: gx: 4 (over z), gy: 8 (over y, x, core).
Axes of the slice: x: 2, y: 2, z: 4, core: 2. Of those that a mesh axis runs over, the one named last changes fastest.
Arguments:
- features: bfloat16 [32768, 256], P(('gx', 'gy')), may hold values from -6 to 6
- self_weight_one: bfloat16 [256, 256], replicated, may hold values from -0.375 to 0.375
- neigh_weight_one: bfloat16 [256, 256], replicated, may hold values from -1.5 to 1.5
- self_weight_two: bfloat16 [256, 256], replicated, may hold values from -0.375 to 0.375
- neigh_weight_two: bfloat16 [256, 256], replicated, may hold values from -1.5 to 1.5
- degree: int32 [32768], P(('gx', 'gy')), may hold values from 128 to 383
- local_tiles: bfloat16 [1024, 128, 128], P(('gx', 'gy')), may hold values from 0 to 1, as said below
- local_coord: int32 [1024, 2], P(('gx', 'gy')), may hold values from 0 to 7, as said below
- local_count: int32 [32], P(('gx', 'gy')), may hold values from 1 to 32, as said below
- send_block: int32 [256], P(('gx', 'gy')), may hold values from 0 to 7
- boundary_tiles: bfloat16 [256, 128, 128], P(('gx', 'gy')), may hold values from 0 to 1, as said below
- boundary_row: int32 [256], P(('gx', 'gy')), may hold values from 0 to 7
- hub_rows: int32 [256], P(('gx', 'gy')), may hold values from 0 to 1023
- hub_tiles: bfloat16 [256, 128, 128], P(('gx', 'gy')), may hold values from 0 to 1, as said below
- hub_coord: int32 [256, 2], P(('gx', 'gy')), may hold values from 0 to 7, as said below
Outputs:
- node_out: bfloat16 [32768, 256], P(('gx', 'gy'))
Inputs may be any that keep to these rules, and one draw needn't show every extreme that they name: `local_tiles`: entries are 0 or 1. `boundary_tiles`: entries are 0 or 1. `hub_tiles`: entries are 0 or 1. `local_coord`: both columns are row blocks of the same device. `local_count`: some device has all 32 slots live. `hub_coord`: column 0 is a row block below 8, column 1 a hub block below 2.
All inputs are finite; a program needn't handle non-finite values.
Results may differ from a plain program's by a relative error of at most 0.005.
Values may be sent and summed in bfloat16 or wider, within the bound.
A program may use at most 64 MiB of HBM per device.

v0:
```python
import jax
import jax.numpy as jnp
from jax import lax
from jax.sharding import PartitionSpec as P


def tile_sum(tiles, rows, sources, weight, block_count):
    product = jnp.einsum("kij,kjf->kif", tiles, sources, preferred_element_type=jnp.float32)
    onehot = (rows[None, :] == jnp.arange(block_count, dtype=jnp.int32)[:, None]).astype(
        jnp.float32
    ) * weight[None, :]
    flat = product.reshape(product.shape[0], -1)
    merged = jnp.dot(onehot, flat, precision=lax.Precision.HIGHEST)
    return merged.reshape(block_count, product.shape[1], product.shape[2])


def layer(
    nodes_in,
    self_weight,
    neigh_weight,
    degree,
    local_tiles,
    local_coord,
    local_count,
    send_block,
    boundary_tiles,
    boundary_row,
    hub_rows,
    hub_tiles,
    hub_coord,
):
    node_count, feat_width = nodes_in.shape
    tile_size = local_tiles.shape[1]
    block_count = node_count // tile_size
    blocks = nodes_in.reshape(block_count, tile_size, feat_width)
    own_hubs = jnp.take(nodes_in, hub_rows, axis=0)
    inner = lax.all_gather(own_hubs, "gy", axis=0, tiled=True)
    hub_feats = lax.all_gather(inner, "gx", axis=0, tiled=True)
    outgoing = jnp.take(blocks, send_block, axis=0)
    incoming = lax.all_to_all(outgoing, "gy", split_axis=0, concat_axis=0, tiled=True)
    live_mask = (jnp.arange(local_tiles.shape[0], dtype=jnp.int32) < local_count[0]).astype(
        jnp.float32
    )
    sources = jnp.take(blocks, local_coord[:, 1], axis=0)
    totals = tile_sum(local_tiles, local_coord[:, 0], sources, live_mask, block_count)
    totals = totals + tile_sum(
        boundary_tiles,
        boundary_row,
        incoming,
        jnp.ones((boundary_tiles.shape[0],), jnp.float32),
        block_count,
    )
    hub_blocks = hub_feats.reshape(-1, tile_size, feat_width)
    hub_sources = jnp.take(hub_blocks, hub_coord[:, 1], axis=0)
    totals = totals + tile_sum(
        hub_tiles,
        hub_coord[:, 0],
        hub_sources,
        jnp.ones((hub_tiles.shape[0],), jnp.float32),
        block_count,
    )
    neigh = (totals.reshape(node_count, feat_width) / degree[:, None].astype(jnp.float32)).astype(
        jnp.bfloat16
    )
    linear = jnp.dot(nodes_in, self_weight, preferred_element_type=jnp.float32)
    return linear + jnp.dot(neigh, neigh_weight, preferred_element_type=jnp.float32)


def per_device(
    features,
    self_weight_one,
    neigh_weight_one,
    self_weight_two,
    neigh_weight_two,
    degree,
    local_tiles,
    local_coord,
    local_count,
    send_block,
    boundary_tiles,
    boundary_row,
    hub_rows,
    hub_tiles,
    hub_coord,
):
    graph = (
        degree,
        local_tiles,
        local_coord,
        local_count,
        send_block,
        boundary_tiles,
        boundary_row,
        hub_rows,
        hub_tiles,
        hub_coord,
    )
    linear_one = layer(features, self_weight_one, neigh_weight_one, *graph)
    relu_one = jnp.maximum(linear_one, 0.0)
    scale = lax.rsqrt(jnp.mean(relu_one * relu_one, axis=-1, keepdims=True) + 1e-06)
    hidden = (relu_one * scale).astype(jnp.bfloat16)
    linear_two = layer(hidden, self_weight_two, neigh_weight_two, *graph)
    return linear_two.astype(jnp.bfloat16)


def solution(mesh):
    placed = (
        P(("gx", "gy"), None),
        P(),
        P(),
        P(),
        P(),
        P(("gx", "gy")),
        P(("gx", "gy"), None, None),
        P(("gx", "gy"), None),
        P(("gx", "gy")),
        P(("gx", "gy")),
        P(("gx", "gy"), None, None),
        P(("gx", "gy")),
        P(("gx", "gy")),
        P(("gx", "gy"), None, None),
        P(("gx", "gy"), None),
    )
    return jax.shard_map(
        per_device, mesh=mesh, in_specs=placed, out_specs=P(("gx", "gy"), None), check_vma=False
    )
```

profile of v0, /device:TPU:0, one launch (start us, length us, event | category | flops | bytes accessed | tf_op | source)
XLA Modules:
  0.0 126.4 jit_solution(13274462036618419214)
XLA Ops:
  1.5 1.6 %gather_fusion.1 = bf16[8,128,256]{2,1,0:T(8,128)(2,1)S(1)} fusion(bf16[8,128,256]{2,1,0:T(8,128)(2,1)} %bitcast.127, s32[1024]{0:T(1024)S(1)} %pad_clamp_fusion.2), kind=kCustom, calls=%fused_computation.1.clone | custom fusion | bytes 1048608 | tf_op jit(solution)/shard_map/jit(_take)/gather | solution.py:39
  3.4 0.9 broadcast_select_fusion.1
  4.3 5.2 %all-to-all-start = ((bf16[8,128,256]{1,2,0:T(8,128)(2,1)}), bf16[8,128,256]{1,2,0:T(8,128)(2,1)S(1)}, u32[]{:S(2)}, u32[]{:S(2)}) async-start(bf16[8,128,256]{1,2,0:T(8,128)(2,1)} %broadcast_select_fusion.1), calls=%async_computation | async-start | bytes 1048576 | tf_op jit(solution)/shard_map/all_to_all | solution.py:40
  10.1 2.0 %gather_fusion = bf16[32,128,256]{2,1,0:T(8,128)(2,1)} fusion(bf16[8,128,256]{2,1,0:T(8,128)(2,1)S(1)} %bitcast.128, s32[1024]{0:T(1024)S(1)} %pad_clamp_fusion.3), kind=kCustom, calls=%fused_computation.clone | custom fusion | bytes 4194432 | tf_op jit(solution)/shard_map/jit(_take)/gather | solution.py:44
  12.2 4.4 %convolution_bitcast_fusion.1 = f32[32,128,256]{1,2,0:T(8,128)} fusion(bf16[32,128,128]{2,1,0:T(8,128)(2,1)S(1)} %copy-done, bf16[32,128,256]{2,1,0:T(8,128)(2,1)} %gather_fusion, pred[32]{0:T(512)(128)(4,1)S(1)} %get-tuple-element.10), kind=kOutput, calls=%fused_computation.15 | convolution fusion | flops 269484032 | bytes 7340064 | tf_op jit(solution)/shard_map/kij,kjf->kif/dot_general | solution.py:8
  16.6 5.4 %copy.38 = f32[4,8,128,256]{3,1,2,0:T(8,128)} copy(f32[4,8,128,256]{2,3,1,0:T(8,128)} %bitcast.130) | data formatting | bytes 8388608
  23.9 9.6 %all_gather.12 = bf16[64,256]{1,0:T(8,128)(2,1)S(1)} all-gather(bf16[8,256]{1,0:T(8,128)(2,1)S(1)} %broadcast_select_fusion.3), channel_id=1, replica_groups=mesh['gx'=4,'gy'=8] {'gy'}, dimensions={0}, use_global_device_ids=true | all-gather | bytes 36864 | tf_op jit(solution)/shard_map/all_gather | solution.py:37
  33.5 13.6 %all_gather.13 = bf16[256,256]{1,0:T(8,128)(2,1)S(1)} all-gather(bf16[64,256]{1,0:T(8,128)(2,1)S(1)} %all_gather.12), channel_id=1, replica_groups=mesh['gx'=4,'gy'=8] {'gx'}, dimensions={0}, use_global_device_ids=true | all-gather | bytes 163840 | tf_op jit(solution)/shard_map/all_gather | solution.py:38
  47.6 1.4 %gather_fusion.3 = bf16[8,128,256]{2,1,0:T(8,128)(2,1)} fusion(bf16[2,128,256]{2,1,0:T(8,128)(2,1)S(1)} %bitcast.135, s32[1024]{0:T(1024)S(1)} %pad_clamp_fusion), kind=kCustom, calls=%fused_computation.3.clone | custom fusion | bytes 1048608 | tf_op jit(solution)/shard_map/jit(_take)/gather | solution.py:54
  49.0 1.5 %convolution_bitcast_fusion.4 = f32[8,128,256]{1,2,0:T(8,128)S(1)} fusion(bf16[8,128,128]{2,1,0:T(8,128)(2,1)} %param.36, bf16[8,128,256]{2,1,0:T(8,128)(2,1)} %gather_fusion.3, pred[8]{0:T(512)(128)(4,1)} %get-tuple-element.6), kind=kOutput, calls=%fused_computation.27 | convolution fusion | flops 67371008 | bytes 1835016 | tf_op jit(solution)/shard_map/kij,kjf->kif/dot_general | solution.py:8
  50.6 1.4 %copy.22 = f32[8,128,256]{2,1,0:T(8,128)} copy(f32[8,128,256]{1,2,0:T(8,128)S(1)} %convolution_bitcast_fusion.4) | data formatting | bytes 2097152 | tf_op jit(solution)/shard_map/kij,kjf->kif/dot_general | solution.py:8
  52.6 1.2 slice_bitcast_fusion
  53.8 1.3 %fusion.64 = f32[1024,256]{1,0:T(8,128)} fusion(bf16[1024,256]{1,0:T(8,128)(2,1)S(1)} %copy-done.1, bf16[256,256]{1,0:T(8,128)(2,1)S(1)} %copy-done.8), kind=kOutput, calls=%fused_computation.101 | convolution fusion | flops 134217728 | bytes 1703936 | tf_op jit(solution)/shard_map/dot_general | solution.py:65
  55.4 1.3 %copy.20 = f32[8,128,256]{2,1,0:T(8,128)} copy(f32[8,128,256]{1,2,0:T(8,128)S(1)} %convolution_bitcast_fusion.5) | data formatting | bytes 2097152 | tf_op jit(solution)/shard_map/kij,kjf->kif/dot_general | solution.py:8
  56.7 2.5 %fusion.35 = f32[8,128,256]{2,0,1:T(8,128)S(1)} fusion(s32[8]{0:T(128)} %param.34, f32[1,8,128,256]{3,2,1,0:T(8,128)} %bitcast.131), kind=kOutput, calls=%fused_computation.64 | convolution fusion | flops 25165888 | bytes 2097184 | tf_op jit(solution)/shard_map/dot_general | solution.py:13
  59.2 3.8 %fusion.10 = f32[8,128,256]{2,0,1:T(8,128)S(1)} fusion(f32[8,128,256]{2,0,1:T(8,128)S(1)} %fusion.35, f32[32]{0:T(128)S(1)} %copy-done.21, s32[32]{0:T(128)S(1)} %copy-done.19, f32[4,8,128,256]{3,1,2,0:T(8,128)} %copy.38), kind=kOutput, calls=%fused_computation.20 | convolution fusion | flops 100925952 | bytes 6291712 | tf_op jit(solution)/shard_map/dot_general | solution.py:13
  63.1 1.2 convolution_add_fusion.3
  65.5 2.0 %gather_fusion.4 = bf16[32,128,256]{2,1,0:T(8,128)(2,1)} fusion(bf16[8,128,256]{2,1,0:T(8,128)(2,1)S(1)} %bitcast.125, s32[1024]{0:T(1024)S(1)} %pad_clamp_fusion.3), kind=kCustom, calls=%fused_computation.4.clone | custom fusion | bytes 4194432 | tf_op jit(solution)/shard_map/jit(_take)/gather | solution.py:44
  68.8 4.4 %convolution_bitcast_fusion = f32[32,128,256]{1,2,0:T(8,128)} fusion(bf16[32,128,128]{2,1,0:T(8,128)(2,1)S(1)} %copy-done, bf16[32,128,256]{2,1,0:T(8,128)(2,1)} %gather_fusion.4, pred[32]{0:T(512)(128)(4,1)S(1)} %copy-done.24), kind=kOutput, calls=%fused_computation.14 | convolution fusion | flops 269484032 | bytes 7340064 | tf_op jit(solution)/shard_map/kij,kjf->kif/dot_general | solution.py:8
  73.3 5.4 %copy.41 = f32[4,8,128,256]{3,1,2,0:T(8,128)} copy(f32[4,8,128,256]{2,3,1,0:T(8,128)} %bitcast.129) | data formatting | bytes 8388608
  79.9 3.5 %all-to-all-start.1 = ((bf16[8,128,256]{1,2,0:T(8,128)(2,1)}), bf16[8,128,256]{1,2,0:T(8,128)(2,1)S(1)}, u32[]{:S(2)}, u32[]{:S(2)}) async-start(bf16[8,128,256]{1,2,0:T(8,128)(2,1)} %broadcast_select_fusion), calls=%async_computation.1 | async-start | bytes 1048576 | tf_op jit(solution)/shard_map/all_to_all | solution.py:40
  83.5 12.9 %all_gather.14 = bf16[64,256]{1,0:T(8,128)(2,1)S(1)} all-gather(bf16[8,256]{1,0:T(8,128)(2,1)S(1)} %broadcast_select_fusion.2), channel_id=1, replica_groups=mesh['gx'=4,'gy'=8] {'gy'}, dimensions={0}, use_global_device_ids=true | all-gather | bytes 36864 | tf_op jit(solution)/shard_map/all_gather | solution.py:37
  96.3 13.6 %all_gather.15 = bf16[256,256]{1,0:T(8,128)(2,1)S(1)} all-gather(bf16[64,256]{1,0:T(8,128)(2,1)S(1)} %all_gather.14), channel_id=1, replica_groups=mesh['gx'=4,'gy'=8] {'gx'}, dimensions={0}, use_global_device_ids=true | all-gather | bytes 163840 | tf_op jit(solution)/shard_map/all_gather | solution.py:38
  109.9 1.4 %gather_fusion.7 = bf16[8,128,256]{2,1,0:T(8,128)(2,1)} fusion(bf16[2,128,256]{2,1,0:T(8,128)(2,1)S(1)} %bitcast.136, s32[1024]{0:T(1024)S(1)} %pad_clamp_fusion), kind=kCustom, calls=%fused_computation.7.clone | custom fusion | bytes 1048608 | tf_op jit(solution)/shard_map/jit(_take)/gather | solution.py:54
  111.3 1.5 %convolution_bitcast_fusion.2 = f32[8,128,256]{1,2,0:T(8,128)S(1)} fusion(bf16[8,128,128]{2,1,0:T(8,128)(2,1)} %param.36, bf16[8,128,256]{2,1,0:T(8,128)(2,1)} %gather_fusion.7, pred[8]{0:T(512)(128)(4,1)} %get-tuple-element.6), kind=kOutput, calls=%fused_computation.23 | convolution fusion | flops 67371008 | bytes 1835016 | tf_op jit(solution)/shard_map/kij,kjf->kif/dot_general | solution.py:8
  112.8 1.3 %copy.30 = f32[8,128,256]{2,1,0:T(8,128)} copy(f32[8,128,256]{1,2,0:T(8,128)S(1)} %convolution_bitcast_fusion.2) | data formatting | bytes 2097152 | tf_op jit(solution)/shard_map/kij,kjf->kif/dot_general | solution.py:8
  114.2 1.3 %fusion.65 = f32[1024,256]{1,0:T(8,128)} fusion(bf16[1024,256]{1,0:T(8,128)(2,1)S(1)} %multiply_convert_fusion, bf16[256,256]{1,0:T(8,128)(2,1)S(1)} %copy-done.9), kind=kOutput, calls=%fused_computation.102 | convolution fusion | flops 134217728 | bytes 1703936 | tf_op jit(solution)/shard_map/dot_general | solution.py:65
  115.8 1.3 %copy.28 = f32[8,128,256]{2,1,0:T(8,128)} copy(f32[8,128,256]{1,2,0:T(8,128)S(1)} %convolution_bitcast_fusion.3) | data formatting | bytes 2097152 | tf_op jit(solution)/shard_map/kij,kjf->kif/dot_general | solution.py:8
  117.1 2.5 %fusion.33 = f32[8,128,256]{2,0,1:T(8,128)S(1)} fusion(s32[8]{0:T(128)S(1)} %copy-done.12, f32[1,8,128,256]{3,2,1,0:T(8,128)} %bitcast.132), kind=kOutput, calls=%fused_computation.63 | convolution fusion | flops 25165888 | bytes 2097184 | tf_op jit(solution)/shard_map/dot_general | solution.py:13
  119.6 3.8 %fusion.13 = f32[8,128,256]{2,0,1:T(8,128)S(1)} fusion(f32[8,128,256]{2,0,1:T(8,128)S(1)} %fusion.33, f32[32]{0:T(128)S(1)} %copy-done.22, s32[32]{0:T(128)S(1)} %copy-done.20, f32[4,8,128,256]{3,1,2,0:T(8,128)} %copy.41), kind=kOutput, calls=%fused_computation.21 | convolution fusion | flops 100925952 | bytes 6291712 | tf_op jit(solution)/shard_map/dot_general | solution.py:13
  123.5 1.2 convolution_add_fusion.2
  125.3 1.1 fusion.17
  (88 shorter events, 9.7 us)
Async XLA Ops:
  0.0 12.2 %copy-start = (bf16[32,128,128]{2,1,0:T(8,128)(2,1)S(1)}, bf16[32,128,128]{2,1,0:T(8,128)(2,1)}, u32[]{:S(2)}) copy-start(bf16[32,128,128]{2,1,0:T(8,128)(2,1)} %param.29) | copy-start | bytes 3145732
  0.0 10.1 %copy-start.1 = (bf16[1024,256]{1,0:T(8,128)(2,1)S(1)}, bf16[1024,256]{1,0:T(8,128)(2,1)}, u32[]{:S(2)}) copy-start(bf16[1024,256]{1,0:T(8,128)(2,1)} %param.23) | copy-start | bytes 1572868
  0.0 9.5 %copy-start.25 = (s32[32,2]{0,1:T(2,128)S(1)}, s32[32,2]{0,1:T(2,128)}, u32[]{:S(2)}) copy-start(s32[32,2]{0,1:T(2,128)} %param.30) | copy-start | bytes 772
  0.0 10.1 %copy-start.27 = (s32[8]{0:T(128)S(1)}, s32[8]{0:T(128)}, u32[]{:S(2)}) copy-start(s32[8]{0:T(128)} %param.35) | copy-start | bytes 100
  1.5 2.8 %copy-start.13 = (pred[8]{0:T(512)(128)(4,1)}, pred[8]{0:T(512)(128)(4,1)S(1)}, u32[]{:S(2)}) copy-start(pred[8]{0:T(512)(128)(4,1)S(1)} %compare_and_fusion.2) | copy-start | bytes 28
  4.3 50.8 %all-to-all-start = ((bf16[8,128,256]{1,2,0:T(8,128)(2,1)}), bf16[8,128,256]{1,2,0:T(8,128)(2,1)S(1)}, u32[]{:S(2)}, u32[]{:S(2)}) async-start(bf16[8,128,256]{1,2,0:T(8,128)(2,1)} %broadcast_select_fusion.1), calls=%async_computation | async-start | bytes 1048576 | tf_op jit(solution)/shard_map/all_to_all | solution.py:40
  9.5 7.1 %copy-start.23 = (pred[32]{0:T(512)(128)(4,1)}, pred[32]{0:T(512)(128)(4,1)S(1)}, u32[]{:S(2)}) copy-start(pred[32]{0:T(512)(128)(4,1)S(1)} %get-tuple-element.10) | copy-start | bytes 100
  10.1 13.8 %copy-start.15 = (pred[8]{0:T(512)(128)(4,1)}, pred[8]{0:T(512)(128)(4,1)S(1)}, u32[]{:S(2)}) copy-start(pred[8]{0:T(512)(128)(4,1)S(1)} %compare_and_fusion.1) | copy-start | bytes 28
  16.6 30.5 %copy-start.26 = (s32[8,2]{0,1:T(2,128)S(1)}, s32[8,2]{0,1:T(2,128)}, u32[]{:S(2)}) copy-start(s32[8,2]{0,1:T(2,128)} %param.37) | copy-start | bytes 196
  22.0 31.7 %copy-start.8 = (bf16[256,256]{1,0:T(8,128)(2,1)S(1)}, bf16[256,256]{1,0:T(8,128)(2,1)}, u32[]{:S(2)}) copy-start(bf16[256,256]{1,0:T(8,128)(2,1)} %param.24) | copy-start | bytes 393220
  22.0 33.0 %copy-start.6 = (bf16[8,128,128]{2,1,0:T(8,128)(2,1)S(1)}, bf16[8,128,128]{2,1,0:T(8,128)(2,1)}, u32[]{:S(2)}) copy-start(bf16[8,128,128]{2,1,0:T(8,128)(2,1)} %param.33) | copy-start | bytes 786436
  23.3 27.3 %copy-start.11 = (s32[1024]{0:T(1024)}, s32[1024]{0:T(1024)S(1)}, u32[]{:S(2)}) copy-start(s32[1024]{0:T(1024)S(1)} %pad_clamp_fusion.1) | copy-start | bytes 12292
  55.0 4.1 %copy-start.19 = (s32[32]{0:T(128)S(1)}, s32[32]{0:T(128)}, u32[]{:S(2)}) copy-start(s32[32]{0:T(128)} %slice_bitcast_fusion.1) | copy-start | bytes 388
  55.0 4.1 %copy-start.21 = (f32[32]{0:T(128)S(1)}, f32[32]{0:T(128)}, u32[]{:S(2)}) copy-start(f32[32]{0:T(128)} %compare_convert_fusion) | copy-start | bytes 388
  56.7 6.4 %copy-start.3 = (f32[8,128,256]{2,1,0:T(8,128)S(1)}, f32[8,128,256]{2,1,0:T(8,128)}, u32[]{:S(2)}) copy-start(f32[8,128,256]{2,1,0:T(8,128)} %copy.22) | copy-start | bytes 3145732
  56.7 6.4 %copy-start.17 = (s32[8]{0:T(128)S(1)}, s32[8]{0:T(128)}, u32[]{:S(2)}) copy-start(s32[8]{0:T(128)} %slice_bitcast_fusion) | copy-start | bytes 100
  63.0 1.8 %copy-start.5 = (f32[1024,256]{1,0:T(8,128)S(1)}, f32[1024,256]{1,0:T(8,128)}, u32[]{:S(2)}) copy-start(f32[1024,256]{1,0:T(8,128)} %fusion.64) | copy-start | bytes 3145732
  63.0 1.8 %copy-start.10 = (bf16[256,256]{1,0:T(8,128)(2,1)S(1)}, bf16[256,256]{1,0:T(8,128)(2,1)}, u32[]{:S(2)}) copy-start(bf16[256,256]{1,0:T(8,128)(2,1)} %param.25) | copy-start | bytes 393220
  64.9 4.0 %copy-start.24 = (pred[32]{0:T(512)(128)(4,1)S(1)}, pred[32]{0:T(512)(128)(4,1)}, u32[]{:S(2)}) copy-start(pred[32]{0:T(512)(128)(4,1)} %copy-done.23) | copy-start | bytes 100
  73.3 5.7 %copy-start.14 = (pred[8]{0:T(512)(128)(4,1)S(1)}, pred[8]{0:T(512)(128)(4,1)}, u32[]{:S(2)}) copy-start(pred[8]{0:T(512)(128)(4,1)} %copy-done.13) | copy-start | bytes 28
  73.3 10.1 %copy-start.16 = (pred[8]{0:T(512)(128)(4,1)S(1)}, pred[8]{0:T(512)(128)(4,1)}, u32[]{:S(2)}) copy-start(pred[8]{0:T(512)(128)(4,1)} %copy-done.15) | copy-start | bytes 28
  78.7 35.5 %copy-start.9 = (bf16[256,256]{1,0:T(8,128)(2,1)S(1)}, bf16[256,256]{1,0:T(8,128)(2,1)}, u32[]{:S(2)}) copy-start(bf16[256,256]{1,0:T(8,128)(2,1)} %param.26) | copy-start | bytes 393220
  79.9 35.6 %all-to-all-start.1 = ((bf16[8,128,256]{1,2,0:T(8,128)(2,1)}), bf16[8,128,256]{1,2,0:T(8,128)(2,1)S(1)}, u32[]{:S(2)}, u32[]{:S(2)}) async-start(bf16[8,128,256]{1,2,0:T(8,128)(2,1)} %broadcast_select_fusion), calls=%async_computation.1 | async-start | bytes 1048576 | tf_op jit(solution)/shard_map/all_to_all | solution.py:40
  112.8 4.3 %copy-start.12 = (s32[8]{0:T(128)S(1)}, s32[8]{0:T(128)}, u32[]{:S(2)}) copy-start(s32[8]{0:T(128)} %param.34) | copy-start | bytes 100
  114.2 5.4 %copy-start.20 = (s32[32]{0:T(128)S(1)}, s32[32]{0:T(128)}, u32[]{:S(2)}) copy-start(s32[32]{0:T(128)} %slice_bitcast_fusion.1) | copy-start | bytes 388
  114.2 5.4 %copy-start.22 = (f32[32]{0:T(128)S(1)}, f32[32]{0:T(128)}, u32[]{:S(2)}) copy-start(f32[32]{0:T(128)} %compare_convert_fusion) | copy-start | bytes 388
  117.1 6.4 %copy-start.2 = (f32[8,128,256]{2,1,0:T(8,128)S(1)}, f32[8,128,256]{2,1,0:T(8,128)}, u32[]{:S(2)}) copy-start(f32[8,128,256]{2,1,0:T(8,128)} %copy.30) | copy-start | bytes 3145732
  117.1 6.4 %copy-start.18 = (s32[8]{0:T(128)S(1)}, s32[8]{0:T(128)}, u32[]{:S(2)}) copy-start(s32[8]{0:T(128)} %slice_bitcast_fusion) | copy-start | bytes 100
  123.4 1.8 %copy-start.4 = (f32[1024,256]{1,0:T(8,128)S(1)}, f32[1024,256]{1,0:T(8,128)}, u32[]{:S(2)}) copy-start(f32[1024,256]{1,0:T(8,128)} %fusion.65) | copy-start | bytes 3145732
  123.5 1.8 %copy-start.7 = (bf16[256,256]{1,0:T(8,128)(2,1)S(1)}, bf16[256,256]{1,0:T(8,128)(2,1)}, u32[]{:S(2)}) copy-start(bf16[256,256]{1,0:T(8,128)(2,1)} %param.27) | copy-start | bytes 393220
where the time goes:
time: 127 us; the launch traced here: 126 us
  blocking collectives  49.6 us (39%)
  matrix products  31.6 us (25%)
  local copies, waits for them, and re-layouts  29.5 us (23%)
  starting transfers between devices  8.67 us (7%)
  other arithmetic  5.83 us (5%)
    all_gather x2, blocking collectives, layer(): hub_feats = lax.all_gather(inner, 'gx', axis=0, tiled=True)  27.1 us
    all_gather x2, blocking collectives, layer(): inner = lax.all_gather(own_hubs, 'gy', axis=0, tiled=True)  22.4 us
    dot_general x6, matrix products, tile_sum(): merged = jnp.dot(onehot, flat, precision=lax.Precision.HIGHEST)  15 us
    dot_general x6, matrix products, tile_sum(): jnp.einsum('kij,kjf->kif', tiles, sources, preferred_element_type=jnp.flo...  12.5 us
    unnamed x58, local copies, waits for them, and re-layouts  11 us
    all_to_all x2, starting transfers between devices, layer(): lax.all_to_all(outgoing, 'gy', split_axis=0, concat_axis=0, tiled=True)  8.67 us
    dot_general x4, local copies, waits for them, and re-layouts, tile_sum(): jnp.einsum('kij,kjf->kif', tiles, sources, preferred_element_type=jnp.flo...  5.27 us
    gather x2, local copies, waits for them, and re-layouts, layer(): sources = jnp.take(blocks, local_coord[:, 1], axis=0)  4.08 us
  transfers between devices with their start and end apart: 2, of which 0 were waited for; matrix products, arithmetic and copies ran while one was open for 22% of the time, Pallas kernels for 0%

commit v1 on v0

--- a/solution.py
+++ b/solution.py
@@ -2,6 +2,19 @@
 import jax.numpy as jnp
 from jax import lax
 from jax.sharding import PartitionSpec as P
+
+
+def collect(shard, axis, dim):
+    ways = lax.axis_size(axis)
+    up = [(d, (d + 1) % ways) for d in range(ways)]
+    down = [(d, (d - 1) % ways) for d in range(ways)]
+    earlier, later = ([shard], [shard])
+    for _ in range(ways // 2):
+        earlier.append(lax.ppermute(earlier[-1], axis, up))
+    for _ in range((ways - 1) // 2):
+        later.append(lax.ppermute(later[-1], axis, down))
+    line = jnp.concatenate([*earlier[::-1], *later[1:]], axis=dim)
+    return jnp.roll(line, (lax.axis_index(axis) - ways // 2) * shard.shape[dim], axis=dim)
 
 
 def tile_sum(tiles, rows, sources, weight, block_count):
@@ -35,7 +48,7 @@
     blocks = nodes_in.reshape(block_count, tile_size, feat_width)
     own_hubs = jnp.take(nodes_in, hub_rows, axis=0)
     inner = lax.all_gather(own_hubs, "gy", axis=0, tiled=True)
-    hub_feats = lax.all_gather(inner, "gx", axis=0, tiled=True)
+    hub_feats = collect(inner, "gx", 0)
     outgoing = jnp.take(blocks, send_block, axis=0)
     incoming = lax.all_to_all(outgoing, "gy", split_axis=0, concat_axis=0, tiled=True)
     live_mask = (jnp.arange(local_tiles.shape[0], dtype=jnp.int32) < local_count[0]).astype(

time: 127 us -> 97.3 us (0.77)
  blocking collectives: 49.6 us -> 20 us
  starting transfers between devices: 8.67 us -> 14.8 us
  local copies, waits for them, and re-layouts: 29.5 us -> 25.4 us
  matrix products: 31.6 us -> 28.8 us
    all_gather x2 -> x0, blocking collectives: 27.1 us -> none  [layer(): hub_feats = lax.all_gather(inner, 'gx', axis=0, tiled=True)]
    ppermute x0 -> x6, starting transfers between devices: none -> 7.76 us  [the longest x2 4.8 us: collect(): later.append(lax.ppermute(later[-1], axis, down))]
    dot_general x6, matrix products: 15 us -> 12.4 us  [tile_sum(): merged = jnp.dot(onehot, flat, precision=lax.Precision.HIGHEST)]
    all_gather x2, blocking collectives: 22.4 us -> 20 us  [layer(): inner = lax.all_gather(own_hubs, 'gy', axis=0, tiled=True)]
    concatenate x0 -> x2, other arithmetic: none -> 2.29 us  [collect(): jnp.roll(line, (lax.axis_index(axis) - ways // 2) * shard.shape[dim], axi...]
    dot_general x4, local copies, waits for them, and re-layouts: 5.27 us -> 3.36 us  [tile_sum(): jnp.einsum('kij,kjf->kif', tiles, sources, preferred_element_type=jnp.flo...]
    eq x2, local copies, waits for them, and re-layouts: 1.72 us -> 0.01 us  [tile_sum(): rows[None, :] == jnp.arange(block_count, dtype=jnp.int32)[:, None]]
    all_to_all x2, starting transfers between devices: 8.67 us -> 6.99 us  [layer(): lax.all_to_all(outgoing, 'gy', split_axis=0, concat_axis=0, tiled=True)]
  transfers between devices with their start and end apart: 2 -> 8, of which waited for: 0 -> 1; matrix products, arithmetic and copies ran while one was open for 22% -> 42% of each run, Pallas kernels for 0% -> 0%
where the time goes in v1:
time: 97.3 us; the launch traced here: 96.6 us
  matrix products  28.8 us (30%)
  local copies, waits for them, and re-layouts  25.4 us (26%)
  blocking collectives  20 us (21%)
  starting transfers between devices  14.8 us (15%)
  other arithmetic  6.42 us (7%)
  between operations  1.15 us (1%)
    all_gather x2, blocking collectives, layer(): inner = lax.all_gather(own_hubs, 'gy', axis=0, tiled=True)  20 us
    dot_general x6, matrix products, tile_sum(): merged = jnp.dot(onehot, flat, precision=lax.Precision.HIGHEST)  12.4 us
    dot_general x6, matrix products, tile_sum(): jnp.einsum('kij,kjf->kif', tiles, sources, preferred_element_type=jnp.flo...  12.1 us
    unnamed x32, local copies, waits for them, and re-layouts  11.1 us
    all_to_all x2, starting transfers between devices, layer(): lax.all_to_all(outgoing, 'gy', split_axis=0, concat_axis=0, tiled=True)  6.99 us
    ppermute x2, starting transfers between devices, collect(): later.append(lax.ppermute(later[-1], axis, down))  4.8 us
    gather x2, local copies, waits for them, and re-layouts, layer(): sources = jnp.take(blocks, local_coord[:, 1], axis=0)  4.07 us
    dot_general x4, local copies, waits for them, and re-layouts, tile_sum(): jnp.einsum('kij,kjf->kif', tiles, sources, preferred_element_type=jnp.flo...  3.36 us
  transfers between devices with their start and end apart: 8, of which 1 were waited for; matrix products, arithmetic and copies ran while one was open for 42% of the time, Pallas kernels for 0%

profile of v1, /device:TPU:0, one launch (start us, length us, event | category | flops | bytes accessed | tf_op | source)
XLA Modules:
  0.0 96.6 jit_solution(10117655263711957254)
XLA Ops:
  1.5 1.7 %gather_fusion.2 = bf16[8,256]{1,0:T(8,128)(2,1)S(1)} fusion(bf16[1024,256]{1,0:T(8,128)(2,1)} %param.25, s32[1024]{0:T(1024)S(1)} %pad_clamp_fusion.1), kind=kCustom, calls=%fused_computation.2.clone | custom fusion | bytes 8224 | tf_op jit(solution)/shard_map/jit(_take)/gather | solution.py:49
  3.2 10.5 %all_gather.6 = bf16[64,256]{1,0:T(8,128)(2,1)S(1)} all-gather(bf16[8,256]{1,0:T(8,128)(2,1)S(1)} %broadcast_select_fusion.3), channel_id=1, replica_groups=mesh['gx'=4,'gy'=8] {'gy'}, dimensions={0}, use_global_device_ids=true | all-gather | bytes 36864 | tf_op jit(solution)/shard_map/all_gather | solution.py:50
  13.8 1.6 %collective-permute-start = (bf16[64,256]{1,0:T(8,128)(2,1)S(1)}, bf16[64,256]{1,0:T(8,128)(2,1)S(1)}, u32[]{:S(2)}, u32[]{:S(2)}) collective-permute-start(bf16[64,256]{1,0:T(8,128)(2,1)S(1)} %all_gather.6), channel_id=1, source_target_pairs={{0,8},{8,16},{16,24},{24,0},{1,9},{9,17},{17,25},{25,1},{2,10},{10... | collective-permute-start | bytes 98312 | tf_op jit(solution)/shard_map/ppermute | solution.py:13
  15.3 2.2 %collective-permute-start.2 = (bf16[64,256]{1,0:T(8,128)(2,1)S(1)}, bf16[64,256]{1,0:T(8,128)(2,1)S(1)}, u32[]{:S(2)}, u32[]{:S(2)}) collective-permute-start(bf16[64,256]{1,0:T(8,128)(2,1)S(1)} %all_gather.6), channel_id=1, source_target_pairs={{0,24},{8,0},{16,8},{24,16},{1,25},{9,1},{17,9},{25,17},{2,26},{10... | collective-permute-start | bytes 98312 | tf_op jit(solution)/shard_map/ppermute | solution.py:15
  17.6 1.7 %gather_fusion.1 = bf16[8,128,256]{2,1,0:T(8,128)(2,1)S(1)} fusion(bf16[8,128,256]{2,1,0:T(8,128)(2,1)} %bitcast.127, s32[1024]{0:T(1024)S(1)} %pad_clamp_fusion.2), kind=kCustom, calls=%fused_computation.1.clone | custom fusion | bytes 1048608 | tf_op jit(solution)/shard_map/jit(_take)/gather | solution.py:52
  19.5 0.9 broadcast_select_fusion.1
  20.5 3.5 %all-to-all-start = ((bf16[8,128,256]{1,2,0:T(8,128)(2,1)}), bf16[8,128,256]{1,2,0:T(8,128)(2,1)S(1)}, u32[]{:S(2)}, u32[]{:S(2)}) async-start(bf16[8,128,256]{1,2,0:T(8,128)(2,1)} %broadcast_select_fusion.1), calls=%async_computation | async-start | bytes 1048576 | tf_op jit(solution)/shard_map/all_to_all | solution.py:53
  24.1 2.0 %gather_fusion = bf16[32,128,256]{2,1,0:T(8,128)(2,1)} fusion(bf16[8,128,256]{2,1,0:T(8,128)(2,1)S(1)} %bitcast.128, s32[1024]{0:T(1024)S(1)} %pad_clamp_fusion.3), kind=kCustom, calls=%fused_computation.clone | custom fusion | bytes 4194432 | tf_op jit(solution)/shard_map/jit(_take)/gather | solution.py:57
  26.1 1.4 %fusion.78 = f32[1024,256]{1,0:T(8,128)} fusion(bf16[1024,256]{1,0:T(8,128)(2,1)S(1)} %copy-done.1, bf16[256,256]{1,0:T(8,128)(2,1)S(1)} %copy-done.8), kind=kOutput, calls=%fused_computation.131 | convolution fusion | flops 134217728 | bytes 1703936 | tf_op jit(solution)/shard_map/dot_general | solution.py:78
  27.5 4.4 %convolution_bitcast_fusion.1 = f32[32,128,256]{1,2,0:T(8,128)} fusion(bf16[32,128,128]{2,1,0:T(8,128)(2,1)S(1)} %copy-done, bf16[32,128,256]{2,1,0:T(8,128)(2,1)} %gather_fusion, pred[32]{0:T(512)(128)(4,1)S(1)} %get-tuple-element.10), kind=kOutput, calls=%fused_computation.15 | convolution fusion | flops 269484032 | bytes 7340064 | tf_op jit(solution)/shard_map/kij,kjf->kif/dot_general | solution.py:21
  32.6 5.5 %copy.38 = f32[4,8,128,256]{3,1,2,0:T(8,128)} copy(f32[4,8,128,256]{2,3,1,0:T(8,128)} %bitcast.129) | data formatting | bytes 8388608
  38.3 1.1 %fusion.38 = bf16[256,256]{1,0:T(8,128)(2,1)S(1)} fusion(s32[]{:T(128)S(6)} %select_n.53, bf16[64,256]{1,0:T(8,128)(2,1)S(1)} %collective-permute-done.1, bf16[64,256]{1,0:T(8,128)(2,1)S(1)} %collective-permute-done, bf16[64,256]{1,0:T(8,128)(2,1)S(1)} %all_gather.6, bf16[64,256]{1,0:T(8,128)(2,1)S(1)} %collective-permute-done.2), kind=kLoop, calls=%fused_computation.74 | loop fusion | flops 1048576 | bytes 262148 | tf_op jit(solution)/shard_map/jit(_roll_dynamic)/concatenate | solution.py:17
  40.0 1.4 %convolution_bitcast_fusion.4 = f32[8,128,256]{1,2,0:T(8,128)S(1)} fusion(bf16[8,128,128]{2,1,0:T(8,128)(2,1)} %param.38, bf16[8,128,256]{2,1,0:T(8,128)(2,1)S(1)} %gather_fusion.3, pred[8]{0:T(512)(128)(4,1)S(1)} %get-tuple-element.6), kind=kOutput, calls=%fused_computation.27 | convolution fusion | flops 67371008 | bytes 1835016 | tf_op jit(solution)/shard_map/kij,kjf->kif/dot_general | solution.py:21
  41.4 1.3 %copy.22 = f32[8,128,256]{2,1,0:T(8,128)} copy(f32[8,128,256]{1,2,0:T(8,128)S(1)} %convolution_bitcast_fusion.4) | data formatting | bytes 2097152 | tf_op jit(solution)/shard_map/kij,kjf->kif/dot_general | solution.py:21
  43.4 1.2 %fusion.49 = f32[8,128,256]{2,0,1:T(8,128)S(1)} fusion(s32[8]{0:T(128)S(1)} %copy-done.12, f32[1,8,128,256]{3,2,1,0:T(8,128)S(1)} %bitcast.131), kind=kOutput, calls=%fused_computation.94 | convolution fusion | flops 25165888 | bytes 2097184 | tf_op jit(solution)/shard_map/dot_general | solution.py:26
  44.6 3.8 %fusion.10 = f32[8,128,256]{2,0,1:T(8,128)S(1)} fusion(f32[8,128,256]{2,0,1:T(8,128)S(1)} %fusion.49, f32[32]{0:T(128)S(1)} %compare_convert_fusion, s32[32]{0:T(128)S(1)} %slice_bitcast_fusion.1, f32[4,8,128,256]{3,1,2,0:T(8,128)} %copy.38), kind=kOutput, calls=%fused_computation.20 | convolution fusion | flops 100925952 | bytes 6291712 | tf_op jit(solution)/shard_map/dot_general | solution.py:26
  48.5 1.2 %convolution_add_fusion.3 = f32[8,128,256]{2,0,1:T(8,128)S(1)} fusion(f32[8,128,256]{2,0,1:T(8,128)S(1)} %fusion.10, s32[8]{0:T(128)S(1)} %slice_bitcast_fusion, f32[1,8,128,256]{3,2,1,0:T(8,128)S(1)} %bitcast.134), kind=kOutput, calls=%fused_computation.30 | convolution fusion | flops 25428032 | bytes 3145760 | tf_op jit(solution)/shard_map/dot_general | solution.py:26
  51.6 9.4 %all_gather.7 = bf16[64,256]{1,0:T(8,128)(2,1)S(1)} all-gather(bf16[8,256]{1,0:T(8,128)(2,1)S(1)} %broadcast_select_fusion.2), channel_id=1, replica_groups=mesh['gx'=4,'gy'=8] {'gy'}, dimensions={0}, use_global_device_ids=true | all-gather | bytes 36864 | tf_op jit(solution)/shard_map/all_gather | solution.py:50
  61.0 1.3 %collective-permute-start.3 = (bf16[64,256]{1,0:T(8,128)(2,1)S(1)}, bf16[64,256]{1,0:T(8,128)(2,1)S(1)}, u32[]{:S(2)}, u32[]{:S(2)}) collective-permute-start(bf16[64,256]{1,0:T(8,128)(2,1)S(1)} %all_gather.7), channel_id=1, source_target_pairs={{0,8},{8,16},{16,24},{24,0},{1,9},{9,17},{17,25},{25,1},{2,10},{10... | collective-permute-start | bytes 98312 | tf_op jit(solution)/shard_map/ppermute | solution.py:13
  62.3 2.6 %collective-permute-start.5 = (bf16[64,256]{1,0:T(8,128)(2,1)S(1)}, bf16[64,256]{1,0:T(8,128)(2,1)S(1)}, u32[]{:S(2)}, u32[]{:S(2)}) collective-permute-start(bf16[64,256]{1,0:T(8,128)(2,1)S(1)} %all_gather.7), channel_id=1, source_target_pairs={{0,24},{8,0},{16,8},{24,16},{1,25},{9,1},{17,9},{25,17},{2,26},{10... | collective-permute-start | bytes 98312 | tf_op jit(solution)/shard_map/ppermute | solution.py:15
  64.8 2.0 %gather_fusion.4 = bf16[32,128,256]{2,1,0:T(8,128)(2,1)} fusion(bf16[8,128,256]{2,1,0:T(8,128)(2,1)S(1)} %bitcast.125, s32[1024]{0:T(1024)S(1)} %pad_clamp_fusion.3), kind=kCustom, calls=%fused_computation.4.clone | custom fusion | bytes 4194432 | tf_op jit(solution)/shard_map/jit(_take)/gather | solution.py:57
  67.5 4.4 %convolution_bitcast_fusion = f32[32,128,256]{1,2,0:T(8,128)} fusion(bf16[32,128,128]{2,1,0:T(8,128)(2,1)S(1)} %copy-done, bf16[32,128,256]{2,1,0:T(8,128)(2,1)} %gather_fusion.4, pred[32]{0:T(512)(128)(4,1)S(1)} %get-tuple-element.10), kind=kOutput, calls=%fused_computation.14 | convolution fusion | flops 269484032 | bytes 7340064 | tf_op jit(solution)/shard_map/kij,kjf->kif/dot_general | solution.py:21
  73.1 3.5 %all-to-all-start.1 = ((bf16[8,128,256]{1,2,0:T(8,128)(2,1)}), bf16[8,128,256]{1,2,0:T(8,128)(2,1)S(1)}, u32[]{:S(2)}, u32[]{:S(2)}) async-start(bf16[8,128,256]{1,2,0:T(8,128)(2,1)} %broadcast_select_fusion), calls=%async_computation.1 | async-start | bytes 1048576 | tf_op jit(solution)/shard_map/all_to_all | solution.py:53
  76.6 1.4 %fusion.79 = f32[1024,256]{1,0:T(8,128)} fusion(bf16[1024,256]{1,0:T(8,128)(2,1)S(1)} %multiply_convert_fusion, bf16[256,256]{1,0:T(8,128)(2,1)S(1)} %copy-done.9), kind=kOutput, calls=%fused_computation.132 | convolution fusion | flops 134217728 | bytes 1703936 | tf_op jit(solution)/shard_map/dot_general | solution.py:78
  78.0 5.5 %copy.41 = f32[4,8,128,256]{3,1,2,0:T(8,128)} copy(f32[4,8,128,256]{2,3,1,0:T(8,128)} %bitcast.130) | data formatting | bytes 8388608
  83.5 1.2 %fusion.31 = bf16[256,256]{1,0:T(8,128)(2,1)S(1)} fusion(s32[]{:T(128)S(6)} %select_n.53, bf16[64,256]{1,0:T(8,128)(2,1)S(1)} %collective-permute-done.4, bf16[64,256]{1,0:T(8,128)(2,1)S(1)} %collective-permute-done.3, bf16[64,256]{1,0:T(8,128)(2,1)S(1)} %all_gather.7, bf16[64,256]{1,0:T(8,128)(2,1)S(1)} %collective-permute-done.5), kind=kLoop, calls=%fused_computation.67 | loop fusion | flops 1048576 | bytes 262148 | tf_op jit(solution)/shard_map/jit(_roll_dynamic)/concatenate | solution.py:17
  85.3 1.4 %convolution_bitcast_fusion.2 = f32[8,128,256]{1,2,0:T(8,128)S(1)} fusion(bf16[8,128,128]{2,1,0:T(8,128)(2,1)} %param.38, bf16[8,128,256]{2,1,0:T(8,128)(2,1)S(1)} %gather_fusion.7, pred[8]{0:T(512)(128)(4,1)S(1)} %get-tuple-element.6), kind=kOutput, calls=%fused_computation.23 | convolution fusion | flops 67371008 | bytes 1835016 | tf_op jit(solution)/shard_map/kij,kjf->kif/dot_general | solution.py:21
  86.7 1.3 %copy.30 = f32[8,128,256]{2,1,0:T(8,128)} copy(f32[8,128,256]{1,2,0:T(8,128)S(1)} %convolution_bitcast_fusion.2) | data formatting | bytes 2097152 | tf_op jit(solution)/shard_map/kij,kjf->kif/dot_general | solution.py:21
  88.7 1.2 %fusion.47 = f32[8,128,256]{2,0,1:T(8,128)S(1)} fusion(s32[8]{0:T(128)S(1)} %copy-done.12, f32[1,8,128,256]{3,2,1,0:T(8,128)S(1)} %bitcast.132), kind=kOutput, calls=%fused_computation.93 | convolution fusion | flops 25165888 | bytes 2097184 | tf_op jit(solution)/shard_map/dot_general | solution.py:26
  89.9 3.8 %fusion.13 = f32[8,128,256]{2,0,1:T(8,128)S(1)} fusion(f32[8,128,256]{2,0,1:T(8,128)S(1)} %fusion.47, f32[32]{0:T(128)S(1)} %compare_convert_fusion, s32[32]{0:T(128)S(1)} %slice_bitcast_fusion.1, f32[4,8,128,256]{3,1,2,0:T(8,128)} %copy.41), kind=kOutput, calls=%fused_computation.21 | convolution fusion | flops 100925952 | bytes 6291712 | tf_op jit(solution)/shard_map/dot_general | solution.py:26
  93.7 1.2 %convolution_add_fusion.2 = f32[8,128,256]{2,0,1:T(8,128)S(1)} fusion(f32[8,128,256]{2,0,1:T(8,128)S(1)} %fusion.13, s32[8]{0:T(128)S(1)} %slice_bitcast_fusion, f32[1,8,128,256]{3,2,1,0:T(8,128)S(1)} %bitcast.133), kind=kOutput, calls=%fused_computation.29 | convolution fusion | flops 25428032 | bytes 3145760 | tf_op jit(solution)/shard_map/dot_general | solution.py:26
  95.5 1.1 %fusion.17 = bf16[1024,256]{1,0:T(8,128)(2,1)} fusion(f32[1024,256]{1,0:T(8,128)S(1)} %copy-done.5, bf16[1024,256]{1,0:T(8,128)(2,1)S(1)} %fusion.18, bf16[256,256]{1,0:T(8,128)(2,1)S(1)} %copy-done.7), kind=kOutput, calls=%fused_computation.31 | convolution fusion | flops 134742016 | bytes 2228224 | tf_op jit(solution)/shard_map/dot_general | solution.py:79
  (72 shorter events, 8.7 us)
Async XLA Ops:
  0.0 27.5 %copy-start = (bf16[32,128,128]{2,1,0:T(8,128)(2,1)S(1)}, bf16[32,128,128]{2,1,0:T(8,128)(2,1)}, u32[]{:S(2)}) copy-start(bf16[32,128,128]{2,1,0:T(8,128)(2,1)} %param.31) | copy-start | bytes 3145732
  0.0 24.0 %copy-start.1 = (bf16[1024,256]{1,0:T(8,128)(2,1)S(1)}, bf16[1024,256]{1,0:T(8,128)(2,1)}, u32[]{:S(2)}) copy-start(bf16[1024,256]{1,0:T(8,128)(2,1)} %param.25) | copy-start | bytes 1572868
  0.0 24.0 %copy-start.13 = (s32[32,2]{0,1:T(2,128)S(1)}, s32[32,2]{0,1:T(2,128)}, u32[]{:S(2)}) copy-start(s32[32,2]{0,1:T(2,128)} %param.32) | copy-start | bytes 772
  0.0 24.0 %copy-start.14 = (s32[8,2]{0,1:T(2,128)S(1)}, s32[8,2]{0,1:T(2,128)}, u32[]{:S(2)}) copy-start(s32[8,2]{0,1:T(2,128)} %param.39) | copy-start | bytes 196
  13.8 18.7 %collective-permute-start = (bf16[64,256]{1,0:T(8,128)(2,1)S(1)}, bf16[64,256]{1,0:T(8,128)(2,1)S(1)}, u32[]{:S(2)}, u32[]{:S(2)}) collective-permute-start(bf16[64,256]{1,0:T(8,128)(2,1)S(1)} %all_gather.6), channel_id=1, source_target_pairs={{0,8},{8,16},{16,24},{24,0},{1,9},{9,17},{17,25},{25,1},{2,10},{10... | collective-permute-start | bytes 98312 | tf_op jit(solution)/shard_map/ppermute | solution.py:13
  15.3 22.8 %collective-permute-start.2 = (bf16[64,256]{1,0:T(8,128)(2,1)S(1)}, bf16[64,256]{1,0:T(8,128)(2,1)S(1)}, u32[]{:S(2)}, u32[]{:S(2)}) collective-permute-start(bf16[64,256]{1,0:T(8,128)(2,1)S(1)} %all_gather.6), channel_id=1, source_target_pairs={{0,24},{8,0},{16,8},{24,16},{1,25},{9,1},{17,9},{25,17},{2,26},{10... | collective-permute-start | bytes 98312 | tf_op jit(solution)/shard_map/ppermute | solution.py:15
  17.6 8.5 %copy-start.8 = (bf16[256,256]{1,0:T(8,128)(2,1)S(1)}, bf16[256,256]{1,0:T(8,128)(2,1)}, u32[]{:S(2)}) copy-start(bf16[256,256]{1,0:T(8,128)(2,1)} %param.26) | copy-start | bytes 393220
  20.5 22.3 %all-to-all-start = ((bf16[8,128,256]{1,2,0:T(8,128)(2,1)}), bf16[8,128,256]{1,2,0:T(8,128)(2,1)S(1)}, u32[]{:S(2)}, u32[]{:S(2)}) async-start(bf16[8,128,256]{1,2,0:T(8,128)(2,1)} %broadcast_select_fusion.1), calls=%async_computation | async-start | bytes 1048576 | tf_op jit(solution)/shard_map/all_to_all | solution.py:53
  32.5 5.8 %collective-permute-start.1 = (bf16[64,256]{1,0:T(8,128)(2,1)S(1)}, bf16[64,256]{1,0:T(8,128)(2,1)S(1)}, u32[]{:S(2)}, u32[]{:S(2)}) collective-permute-start(bf16[64,256]{1,0:T(8,128)(2,1)S(1)} %collective-permute-done), channel_id=1, source_target_pairs={{0,8},{8,16},{16,24},{24,0},{1,9},{9,17},{17,25},{25,1},{2,10},{10... | collective-permute-start | bytes 98312 | tf_op jit(solution)/shard_map/ppermute | solution.py:13
  32.6 5.6 %copy-start.11 = (s32[1024]{0:T(1024)S(1)}, s32[1024]{0:T(1024)}, u32[]{:S(2)}) copy-start(s32[1024]{0:T(1024)} %param.30) | copy-start | bytes 12292
  38.2 4.6 %copy-start.6 = (bf16[8,128,128]{2,1,0:T(8,128)(2,1)S(1)}, bf16[8,128,128]{2,1,0:T(8,128)(2,1)}, u32[]{:S(2)}) copy-start(bf16[8,128,128]{2,1,0:T(8,128)(2,1)} %param.35) | copy-start | bytes 786436
  40.0 3.4 %copy-start.12 = (s32[8]{0:T(128)S(1)}, s32[8]{0:T(128)}, u32[]{:S(2)}) copy-start(s32[8]{0:T(128)} %param.36) | copy-start | bytes 100
  43.4 5.1 %copy-start.3 = (f32[8,128,256]{2,1,0:T(8,128)S(1)}, f32[8,128,256]{2,1,0:T(8,128)}, u32[]{:S(2)}) copy-start(f32[8,128,256]{2,1,0:T(8,128)} %copy.22) | copy-start | bytes 3145732
  48.5 1.8 %copy-start.4 = (f32[1024,256]{1,0:T(8,128)S(1)}, f32[1024,256]{1,0:T(8,128)}, u32[]{:S(2)}) copy-start(f32[1024,256]{1,0:T(8,128)} %fusion.78) | copy-start | bytes 3145732
  48.5 1.8 %copy-start.10 = (bf16[256,256]{1,0:T(8,128)(2,1)S(1)}, bf16[256,256]{1,0:T(8,128)(2,1)}, u32[]{:S(2)}) copy-start(bf16[256,256]{1,0:T(8,128)(2,1)} %param.27) | copy-start | bytes 393220
  61.0 15.6 %collective-permute-start.3 = (bf16[64,256]{1,0:T(8,128)(2,1)S(1)}, bf16[64,256]{1,0:T(8,128)(2,1)S(1)}, u32[]{:S(2)}, u32[]{:S(2)}) collective-permute-start(bf16[64,256]{1,0:T(8,128)(2,1)S(1)} %all_gather.7), channel_id=1, source_target_pairs={{0,8},{8,16},{16,24},{24,0},{1,9},{9,17},{17,25},{25,1},{2,10},{10... | collective-permute-start | bytes 98312 | tf_op jit(solution)/shard_map/ppermute | solution.py:13
  62.3 21.3 %collective-permute-start.5 = (bf16[64,256]{1,0:T(8,128)(2,1)S(1)}, bf16[64,256]{1,0:T(8,128)(2,1)S(1)}, u32[]{:S(2)}, u32[]{:S(2)}) collective-permute-start(bf16[64,256]{1,0:T(8,128)(2,1)S(1)} %all_gather.7), channel_id=1, source_target_pairs={{0,24},{8,0},{16,8},{24,16},{1,25},{9,1},{17,9},{25,17},{2,26},{10... | collective-permute-start | bytes 98312 | tf_op jit(solution)/shard_map/ppermute | solution.py:15
  67.4 9.2 %copy-start.9 = (bf16[256,256]{1,0:T(8,128)(2,1)S(1)}, bf16[256,256]{1,0:T(8,128)(2,1)}, u32[]{:S(2)}) copy-start(bf16[256,256]{1,0:T(8,128)(2,1)} %param.28) | copy-start | bytes 393220
  73.1 15.0 %all-to-all-start.1 = ((bf16[8,128,256]{1,2,0:T(8,128)(2,1)}), bf16[8,128,256]{1,2,0:T(8,128)(2,1)S(1)}, u32[]{:S(2)}, u32[]{:S(2)}) async-start(bf16[8,128,256]{1,2,0:T(8,128)(2,1)} %broadcast_select_fusion), calls=%async_computation.1 | async-start | bytes 1048576 | tf_op jit(solution)/shard_map/all_to_all | solution.py:53
  76.6 7.0 %collective-permute-start.4 = (bf16[64,256]{1,0:T(8,128)(2,1)S(1)}, bf16[64,256]{1,0:T(8,128)(2,1)S(1)}, u32[]{:S(2)}, u32[]{:S(2)}) collective-permute-start(bf16[64,256]{1,0:T(8,128)(2,1)S(1)} %collective-permute-done.3), channel_id=1, source_target_pairs={{0,8},{8,16},{16,24},{24,0},{1,9},{9,17},{17,25},{25,1},{2,10},{10... | collective-permute-start | bytes 98312 | tf_op jit(solution)/shard_map/ppermute | solution.py:13
  88.7 5.1 %copy-start.2 = (f32[8,128,256]{2,1,0:T(8,128)S(1)}, f32[8,128,256]{2,1,0:T(8,128)}, u32[]{:S(2)}) copy-start(f32[8,128,256]{2,1,0:T(8,128)} %copy.30) | copy-start | bytes 3145732
  93.7 1.8 %copy-start.5 = (f32[1024,256]{1,0:T(8,128)S(1)}, f32[1024,256]{1,0:T(8,128)}, u32[]{:S(2)}) copy-start(f32[1024,256]{1,0:T(8,128)} %fusion.79) | copy-start | bytes 3145732
  93.7 1.8 %copy-start.7 = (bf16[256,256]{1,0:T(8,128)(2,1)S(1)}, bf16[256,256]{1,0:T(8,128)(2,1)}, u32[]{:S(2)}) copy-start(bf16[256,256]{1,0:T(8,128)(2,1)} %param.29) | copy-start | bytes 393220
